TPU v7x, 32 devices: a whole 2x2x4 slice. The times are simulated.
32 devices in a mesh: ia: 4 (over z), ja: 4 (over y, core), ka: 2 (over x).
Axes of the slice: x: 2, y: 2, z: 4, core: 2. Of those that a mesh axis runs over, the one named last changes fastest.
Arguments:
- tensor: float32 [8192, 8, 1024], P('ja', 'ka', 'ia'), may hold values from -6 to 6
- factor_a: float32 [1024, 128], P('ia'), may hold values from -1 to 1
- factor_c: float32 [8, 128], P('ka'), may hold values from -2 to 2
- gram_c: float32 [128, 128], replicated, may hold values from -12 to 24, as said below
Outputs:
- factor_b: float32 [8192, 128], P('ja')
- factor_c_new: float32 [8, 128], P('ka')
Inputs may be any that keep to these rules, and one draw needn't show every extreme that they name: `gram_c`: symmetric positive definite.
All inputs are finite; a program needn't handle non-finite values.
Results may differ from a plain program's by a relative error of at most 0.000071.
Values sent between devices are 32-bit elements; how exact they have to be, the bound alone decides.
A program may use at most 64 MiB of HBM per device.

v0:
```python
import jax
import jax.numpy as jnp
from jax import lax
from jax.sharding import PartitionSpec as P


def right_solve(rhs, system):
    lower = jnp.linalg.cholesky(system)
    middle = lax.linalg.triangular_solve(lower, rhs, left_side=False, lower=True, transpose_a=True)
    return lax.linalg.triangular_solve(
        lower, middle, left_side=False, lower=True, transpose_a=False
    )


def body(tensor, factor_a, factor_c, gram_c):
    high = lax.Precision.HIGHEST
    mode_two, mode_three, mode_one = tensor.shape
    rank = factor_a.shape[1]
    gram_a = lax.psum(
        jnp.dot(factor_a.T, factor_a, precision=high, preferred_element_type=jnp.float32), "ia"
    )
    system_b = gram_a * gram_c
    flat = jnp.dot(
        tensor.reshape(mode_two * mode_three, mode_one),
        factor_a,
        precision=high,
        preferred_element_type=jnp.float32,
    )
    partial_value = flat.reshape(mode_two, mode_three, rank)
    mttkrp_b = lax.psum(jnp.sum(partial_value * factor_c[None, :, :], axis=1), ("ia", "ka"))
    factor_b = right_solve(mttkrp_b, system_b)
    mttkrp_c = lax.psum(jnp.sum(partial_value * factor_b[:, None, :], axis=0), ("ia", "ja"))
    gram_b = lax.psum(
        jnp.dot(factor_b.T, factor_b, precision=high, preferred_element_type=jnp.float32), "ja"
    )
    factor_c_new = right_solve(mttkrp_c, gram_a * gram_b)
    return (factor_b, factor_c_new)


def solution(mesh):
    placed = (P("ja", "ka", "ia"), P("ia", None), P("ka", None), P())
    return jax.shard_map(
        body, mesh=mesh, in_specs=placed, out_specs=(P("ja", None), P("ka", None)), check_vma=False
    )
```

profile of v0, /device:TPU:0, one launch (start us, length us, event | category | flops | bytes accessed | tf_op | source)
XLA Modules:
  0.0 200.3 jit_solution(17277993881042223334)
XLA Ops:
  7.2 0.0 copy-start
  7.2 0.0 all-reduce.6.cloned.1.call-start
  7.2 0.8 copy-done
  8.1 1.0 fusion.15
  9.1 0.0 all-reduce.6.cloned.1.call-update
  9.1 0.0 copy-start.3
  9.1 0.0 all-reduce.4.cloned.1.call-start
  9.2 12.6 %multiply_reduce_fusion.1 = (f32[2048,128]{1,0:T(8,128)}, f32[2048,4,128]{2,0,1:T(8,128)}) fusion(f32[4,128]{1,0:T(4,128)} %param.7, f32[256,128]{1,0:T(8,128)S(1)} %copy-done, f32[2048,4,256]{2,1,0:T(4,128)} %param.5), kind=kOutput, calls=%fused_computation.3 | convolution fusion | flops 3223060480 | bytes 13764608 | tf_op jit(solution)/shard_map/dot_general | solution.py:23
  21.8 0.0 all-reduce.4.cloned.1.call-update
  21.8 0.2 all-reduce.8.cloned.1.call-start
  22.0 0.0 copy-done.3
  22.0 0.1 copy.8
  22.1 25.2 %all-reduce.6.cloned.1.call-done = f32[128,128]{0,1:T(8,128)} async-done(((f32[128,128]{0,1:T(8,128)}), f32[128,128]{0,1:T(8,128)}) %all-reduce.6.cloned.1.call-update) | async-done | bytes 65552 | tf_op jit(solution)/shard_map/psum | solution.py:19
  47.3 0.8 mul.24
  48.2 0.1 copy.9
  48.3 11.7 %cholesky.44 = f32[128,128]{1,0:T(8,128)S(1)} custom-call(f32[128,128]{1,0:T(8,128)S(1)} %fusion.14), custom_call_target="Cholesky" | custom-call | tf_op jit(solution)/shard_map/jit(cholesky)/cholesky | solution.py:8
  60.1 0.6 compare_reduce_fusion.1
  60.7 0.7 fusion.3
  61.4 9.8 %custom-call.12 = f32[1,128,128]{1,2,0:T(8,128)S(1)} custom-call(f32[1,128,128]{2,1,0:T(8,128)S(1)} %fusion.3), custom_call_target="InvertDiagBlocksLowerTriangular" | custom-call | tf_op jit(solution)/shard_map/triangular_solve | solution.py:9
  71.2 58.4 %all-reduce.4.cloned.1.call-done = f32[2048,128]{1,0:T(8,128)} async-done(((f32[2048,128]{1,0:T(8,128)}), f32[2048,128]{1,0:T(8,128)}) %all-reduce.4.cloned.1.call-update) | async-done | bytes 1048592 | tf_op jit(solution)/shard_map/psum | solution.py:30
  129.6 2.2 %fusion.12 = f32[2048,128]{1,0:T(8,128)S(1)} fusion(f32[2048,128]{1,0:T(8,128)} %all-reduce.4.cloned.1.call-done, f32[1,128,128]{1,2,0:T(8,128)S(1)} %custom-call.12), kind=kOutput, calls=%fused_computation.17 | convolution fusion | flops 402653184 | bytes 2162688 | tf_op jit(solution)/shard_map/triangular_solve | solution.py:9
  131.8 1.0 fusion.10
  132.8 0.0 copy-start.1
  132.8 0.0 copy-start.2
  132.8 2.4 %fusion.16 = f32[128,128]{0,1:T(8,128)} fusion(f32[2048,128]{1,0:T(8,128)S(1)} %fusion.10), kind=kOutput, calls=%fused_computation.28 | convolution fusion | flops 402653184 | bytes 1114112 | tf_op jit(solution)/shard_map/dot_general | solution.py:34
  135.2 0.0 all-reduce.8.cloned.1.call-update
  135.2 2.5 %multiply_reduce_fusion = f32[4,128]{1,0:T(4,128)S(1)} fusion(f32[2048,4,128]{2,0,1:T(8,128)} %get-tuple-element.4, f32[2048,128]{1,0:T(8,128)S(1)} %fusion.10), kind=kLoop, calls=%fused_computation.2 | loop fusion | flops 2096640 | bytes 5244928 | tf_op jit(solution)/shard_map/reduce_sum | solution.py:32
  137.7 31.2 %psum.30 = f32[4,128]{1,0:T(4,128)S(1)} all-reduce(f32[4,128]{1,0:T(4,128)S(1)} %multiply_reduce_fusion), channel_id=1, replica_groups=mesh['ia'=4,'ja'=4,'ka'=2] {'ia','ja'}, use_global_device_ids=true, to_apply=%region_6.8 | all-reduce | flops 512 | bytes 4096 | tf_op jit(solution)/shard_map/psum | solution.py:32
  169.0 0.0 all-reduce.8.cloned.1.call-done
  169.0 0.0 copy-done.2
  169.0 0.8 mul.27
  169.8 0.1 copy.11
  169.9 11.7 %cholesky.55 = f32[128,128]{1,0:T(8,128)S(1)} custom-call(f32[128,128]{1,0:T(8,128)S(1)} %fusion.9), custom_call_target="Cholesky" | custom-call | tf_op jit(solution)/shard_map/jit(cholesky)/cholesky | solution.py:8
  181.7 0.6 compare_reduce_fusion
  182.3 0.7 fusion.4
  183.0 9.8 %custom-call.13 = f32[1,128,128]{1,2,0:T(8,128)S(1)} custom-call(f32[1,128,128]{2,1,0:T(8,128)S(1)} %fusion.4), custom_call_target="InvertDiagBlocksLowerTriangular" | custom-call | tf_op jit(solution)/shard_map/triangular_solve | solution.py:9
  192.8 0.2 fusion.7
  193.0 0.8 fusion.5
  193.8 0.0 copy-done.1
  (4 shorter events, 0.1 us)
Async XLA Ops:
  7.2 0.9 copy-start
  7.2 40.2 %all-reduce.6.cloned.1.call-start = ((), (), s32[]{:S(2)}) async-start(), calls=%async_computation.1 | async-start | bytes 131072 | tf_op jit(solution)/shard_map/psum | solution.py:19
  9.1 12.9 %copy-start.3 = (f32[128,128]{1,0:T(8,128)S(1)}, f32[128,128]{1,0:T(8,128)}, u32[]{:S(2)}) copy-start(f32[128,128]{1,0:T(8,128)} %param.8) | copy-start | bytes 196612
  9.1 120.5 %all-reduce.4.cloned.1.call-start = ((), (), s32[]{:S(2)}) async-start(), calls=%async_computation | async-start | bytes 2097152 | tf_op jit(solution)/shard_map/psum | solution.py:30
  21.8 147.2 %all-reduce.8.cloned.1.call-start = ((), (), s32[]{:S(2)}) async-start(), calls=%async_computation.2 | async-start | bytes 131072 | tf_op jit(solution)/shard_map/psum | solution.py:33
  132.8 61.0 %copy-start.1 = (f32[2048,128]{1,0:T(8,128)}, f32[2048,128]{1,0:T(8,128)S(1)}, u32[]{:S(2)}) copy-start(f32[2048,128]{1,0:T(8,128)S(1)} %fusion.10) | copy-start | bytes 3145732
  132.8 36.2 %copy-start.2 = (f32[128,128]{0,1:T(8,128)S(1)}, f32[128,128]{0,1:T(8,128)}, u32[]{:S(2)}) copy-start(f32[128,128]{0,1:T(8,128)} %all-reduce.6.cloned.1.call-done) | copy-start | bytes 196612
Sparse Core Ops, SparseCore 0:
  10.3 37.0 all-reduce.5
  51.4 78.1 all-reduce.3
  135.4 31.1 all-reduce.7
where the time goes:
time: 201 us; the launch traced here: 200 us
  waiting for transfers between devices  83.7 us (42%)
  other arithmetic  49.9 us (25%)
  blocking collectives  31.2 us (16%)
  matrix products  20.2 us (10%)
  between operations  13.9 us (7%)
    psum x1, waiting for transfers between devices, body(): lax.psum(jnp.sum(partial_value * factor_c[None, :, :], axis=1), ('ia', 'k...  58.4 us
    psum x1, blocking collectives, body(): lax.psum(jnp.sum(partial_value * factor_b[:, None, :], axis=0), ('ia', 'j...  31.2 us
    psum x1, waiting for transfers between devices, body(): lax.psum(jnp.dot(factor_a.T, factor_a, precision=high, preferred_element_...  25.2 us
    another operation x6, other arithmetic, right_solve(): lower = jnp.linalg.cholesky(system)  24.8 us
    another operation x4, other arithmetic, right_solve(): lax.linalg.triangular_solve(lower, rhs, left_side=False, lower=True, tran...  20.9 us
    dot_general x1, matrix products, body(): jnp.dot(tensor.reshape(mode_two * mode_three, mode_one), factor_a, precis...  12.6 us
  transfers between devices with their start and end apart: 3, of which 2 were waited for; matrix products, arithmetic and copies ran while one was open for 19% of the time, Pallas kernels for 0%

commit v1 on v0

--- a/solution.py
+++ b/solution.py
@@ -27,7 +27,9 @@
         preferred_element_type=jnp.float32,
     )
     partial_value = flat.reshape(mode_two, mode_three, rank)
-    mttkrp_b = lax.psum(jnp.sum(partial_value * factor_c[None, :, :], axis=1), ("ia", "ka"))
+    mttkrp_b = jnp.sum(partial_value * factor_c[None, :, :], axis=1)
+    for c in ("ka", "ia"):
+        mttkrp_b = lax.psum(mttkrp_b, c)
     factor_b = right_solve(mttkrp_b, system_b)
     mttkrp_c = lax.psum(jnp.sum(partial_value * factor_b[:, None, :], axis=0), ("ia", "ja"))
     gram_b = lax.psum(

time: 201 us -> 216 us (1.075)
  waiting for transfers between devices: 83.7 us -> 98.1 us
    psum x2, waiting for transfers between devices: 83.6 us -> 98 us  [body(): mttkrp_b = lax.psum(mttkrp_b, c)]
  transfers between devices with their start and end apart: 3 -> 3, of which waited for: 2 -> 2; matrix products, arithmetic and copies ran while one was open for 19% -> 2% of each run, Pallas kernels for 0% -> 0%
where the time goes in v1:
time: 216 us; the launch traced here: 215 us
  waiting for transfers between devices  98.1 us (45%)
  other arithmetic  49.9 us (23%)
  blocking collectives  31.9 us (15%)
  matrix products  20.2 us (9%)
  between operations  13.9 us (6%)
    psum x2, waiting for transfers between devices, body(): mttkrp_b = lax.psum(mttkrp_b, c)  98 us
    psum x1, blocking collectives, body(): lax.psum(jnp.sum(partial_value * factor_b[:, None, :], axis=0), ('ia', 'j...  31.9 us
    another operation x6, other arithmetic, right_solve(): lower = jnp.linalg.cholesky(system)  24.8 us
    another operation x4, other arithmetic, right_solve(): lax.linalg.triangular_solve(lower, rhs, left_side=False, lower=True, tran...  20.9 us
    dot_general x1, matrix products, body(): jnp.dot(tensor.reshape(mode_two * mode_three, mode_one), factor_a, precis...  12.6 us
  transfers between devices with their start and end apart: 3, of which 2 were waited for; matrix products, arithmetic and copies ran while one was open for 2% of the time, Pallas kernels for 0%

profile of v1, /device:TPU:0, one launch (start us, length us, event | category | flops | bytes accessed | tf_op | source)
XLA Modules:
  0.0 215.4 jit_solution(3703378985220969889)
XLA Ops:
  7.2 0.0 copy-start
  7.2 0.0 copy-start.3
  7.2 0.0 all-reduce.5.cloned.1.call-start
  7.2 0.8 copy-done
  8.1 12.6 %multiply_reduce_fusion.1 = (f32[2048,128]{1,0:T(8,128)}, f32[2048,4,128]{2,0,1:T(8,128)}) fusion(f32[4,128]{1,0:T(4,128)} %param.7, f32[256,128]{1,0:T(8,128)S(1)} %copy-done, f32[2048,4,256]{2,1,0:T(4,128)} %param.5), kind=kOutput, calls=%fused_computation.3 | convolution fusion | flops 3223060480 | bytes 13764608 | tf_op jit(solution)/shard_map/dot_general | solution.py:23
  20.7 0.0 all-reduce.5.cloned.1.call-update
  20.7 0.0 all-reduce.9.cloned.1.call-start
  20.8 1.0 fusion.15
  21.8 41.9 %all-reduce.5.cloned.1.call-done = f32[2048,128]{1,0:T(8,128)} async-done(((f32[2048,128]{1,0:T(8,128)}), f32[2048,128]{1,0:T(8,128)}) %all-reduce.5.cloned.1.call-update) | async-done | bytes 1048592 | tf_op jit(solution)/shard_map/psum | solution.py:32
  63.7 0.0 all-reduce.9.cloned.1.call-update
  63.7 0.2 all-reduce.7.cloned.1.call-start
  63.9 0.0 copy-done.3
  64.0 0.1 copy.8
  64.0 56.1 %all-reduce.9.cloned.1.call-done = (f32[2048,128]{1,0:T(8,128)}, f32[128,128]{0,1:T(8,128)}) async-done(((f32[2048,128]{1,0:T(8,128)}, f32[128,128]{0,1:T(8,128)}), (f32[2048,128]{1,0:T(8,128)}, f32[128,128]{0,1:T(8,128)})) %all-reduce.9.cloned.1.call-update) | async-done | bytes 1114128 | tf_op jit(solution)/shard_map/psum | solution.py:32
  120.2 0.8 mul.24
  121.0 0.1 copy.9
  121.1 11.7 %cholesky.44 = f32[128,128]{1,0:T(8,128)S(1)} custom-call(f32[128,128]{1,0:T(8,128)S(1)} %fusion.14), custom_call_target="Cholesky" | custom-call | tf_op jit(solution)/shard_map/jit(cholesky)/cholesky | solution.py:8
  132.9 0.6 compare_reduce_fusion.1
  133.5 0.7 fusion.3
  134.2 9.8 %custom-call.12 = f32[1,128,128]{1,2,0:T(8,128)S(1)} custom-call(f32[1,128,128]{2,1,0:T(8,128)S(1)} %fusion.3), custom_call_target="InvertDiagBlocksLowerTriangular" | custom-call | tf_op jit(solution)/shard_map/triangular_solve | solution.py:9
  144.0 2.2 %fusion.12 = f32[2048,128]{1,0:T(8,128)S(1)} fusion(f32[2048,128]{1,0:T(8,128)} %get-tuple-element.3, f32[1,128,128]{1,2,0:T(8,128)S(1)} %custom-call.12), kind=kOutput, calls=%fused_computation.17 | convolution fusion | flops 402653184 | bytes 2162688 | tf_op jit(solution)/shard_map/triangular_solve | solution.py:9
  146.2 1.0 fusion.10
  147.2 0.0 copy-start.1
  147.2 0.0 copy-start.2
  147.2 2.4 %fusion.16 = f32[128,128]{0,1:T(8,128)} fusion(f32[2048,128]{1,0:T(8,128)S(1)} %fusion.10), kind=kOutput, calls=%fused_computation.28 | convolution fusion | flops 402653184 | bytes 1114112 | tf_op jit(solution)/shard_map/dot_general | solution.py:36
  149.6 0.0 all-reduce.7.cloned.1.call-update
  149.7 2.5 %multiply_reduce_fusion = f32[4,128]{1,0:T(4,128)S(1)} fusion(f32[2048,4,128]{2,0,1:T(8,128)} %get-tuple-element.6, f32[2048,128]{1,0:T(8,128)S(1)} %fusion.10), kind=kLoop, calls=%fused_computation.2 | loop fusion | flops 2096640 | bytes 5244928 | tf_op jit(solution)/shard_map/reduce_sum | solution.py:34
  152.1 31.9 %psum.38 = f32[4,128]{1,0:T(4,128)S(1)} all-reduce(f32[4,128]{1,0:T(4,128)S(1)} %multiply_reduce_fusion), channel_id=1, replica_groups=mesh['ia'=4,'ja'=4,'ka'=2] {'ia','ja'}, use_global_device_ids=true, to_apply=%region_7.9 | all-reduce | flops 512 | bytes 4096 | tf_op jit(solution)/shard_map/psum | solution.py:34
  184.0 0.0 all-reduce.7.cloned.1.call-done
  184.1 0.0 copy-done.2
  184.1 0.8 mul.27
  184.9 0.1 copy.11
  185.0 11.7 %cholesky.55 = f32[128,128]{1,0:T(8,128)S(1)} custom-call(f32[128,128]{1,0:T(8,128)S(1)} %fusion.9), custom_call_target="Cholesky" | custom-call | tf_op jit(solution)/shard_map/jit(cholesky)/cholesky | solution.py:8
  196.8 0.6 compare_reduce_fusion
  197.4 0.7 fusion.4
  198.1 9.8 %custom-call.13 = f32[1,128,128]{1,2,0:T(8,128)S(1)} custom-call(f32[1,128,128]{2,1,0:T(8,128)S(1)} %fusion.4), custom_call_target="InvertDiagBlocksLowerTriangular" | custom-call | tf_op jit(solution)/shard_map/triangular_solve | solution.py:9
  207.9 0.2 fusion.7
  208.1 0.8 fusion.5
  208.9 0.0 copy-done.1
  (4 shorter events, 0.1 us)
Async XLA Ops:
  7.2 0.9 copy-start
  7.2 56.8 %copy-start.3 = (f32[128,128]{1,0:T(8,128)S(1)}, f32[128,128]{1,0:T(8,128)}, u32[]{:S(2)}) copy-start(f32[128,128]{1,0:T(8,128)} %param.8) | copy-start | bytes 196612
  7.2 56.5 %all-reduce.5.cloned.1.call-start = ((), (), s32[]{:S(2)}) async-start(), calls=%async_computation | async-start | bytes 2097152 | tf_op jit(solution)/shard_map/psum | solution.py:32
  20.7 99.5 %all-reduce.9.cloned.1.call-start = ((), (), s32[]{:S(2)}) async-start(), calls=%async_computation.2 | async-start | bytes 2228224 | tf_op jit(solution)/shard_map/psum | solution.py:32
  63.7 120.3 %all-reduce.7.cloned.1.call-start = ((), (), s32[]{:S(2)}) async-start(), calls=%async_computation.1 | async-start | bytes 131072 | tf_op jit(solution)/shard_map/psum | solution.py:35
  147.2 61.7 %copy-start.1 = (f32[2048,128]{1,0:T(8,128)}, f32[2048,128]{1,0:T(8,128)S(1)}, u32[]{:S(2)}) copy-start(f32[2048,128]{1,0:T(8,128)S(1)} %fusion.10) | copy-start | bytes 3145732
  147.2 36.9 %copy-start.2 = (f32[128,128]{0,1:T(8,128)S(1)}, f32[128,128]{0,1:T(8,128)}, u32[]{:S(2)}) copy-start(f32[128,128]{0,1:T(8,128)} %get-tuple-element.4) | copy-start | bytes 196612
Sparse Core Ops, SparseCore 0:
  20.8 42.8 all-reduce.4
  66.1 53.9 all-reduce.8
  149.8 30.8 all-reduce.6
